TPU v7x, 128 devices: a whole 4x4x4 slice. The times are simulated.
128 devices in a mesh: tm: 4 (over x), panel: 32 (over y, z, core).
Axes of the slice: x: 4, y: 4, z: 4, core: 2. Of those that a mesh axis runs over, the one named last changes fastest.
Arguments:
- separator_cov: float32 [4, 2048, 2048], P('tm', 'panel'), may hold values from -6 to 6
- separator_arrow: float32 [4, 6, 2048], P('tm'), may hold values from -6 to 6
- coupling: float32 [4, 2048, 2048], P('tm', 'panel'), may hold values from -0.25 to 0.25
- arrow_factor: float32 [4, 6, 2048], P('tm'), may hold values from -6 to 6
- arrow_tip: float32 [6, 6], replicated, may hold values from -6 to 6
- inverse_gram: float32 [4, 2048, 2048], P('tm', 'panel'), may hold values from -6 to 6
Outputs:
- diag_cov: float32 [4, 2048, 2048], P('tm', 'panel')
- off_diag: float32 [4, 2048, 2048], P('tm', 'panel')
- arrow_cov: float32 [4, 6, 2048], P('tm', None, 'panel')
All inputs are finite; a program needn't handle non-finite values.
Results may differ from a plain program's by a relative error of at most 0.0001.
Values sent between devices are 32-bit elements; how exact they have to be, the bound alone decides.
No kernel may reach another device: no remote copies, remote signals or barrier semaphores. Data moves between devices by JAX's collectives and lax.ppermute only.
A program may use at most 128 MiB of HBM per device.

v0:
```python
import jax
import jax.numpy as jnp
from jax import lax
from jax.sharding import PartitionSpec as P

hp = lax.Precision.HIGHEST


def passed_along(block, axis, distance):
    devices = range(lax.axis_size(axis))
    route = [(i - distance, i) for i in devices if i - distance in devices]
    return lax.ppermute(block, axis, route)


def matmul(left, right):
    return jnp.dot(left, right, preferred_element_type=jnp.float32, precision=hp)


def inner_rows(left, right):
    return lax.dot_general(
        left, right, (((0,), (0,)), ((), ())), preferred_element_type=jnp.float32, precision=hp
    )


def per_device(separator_cov, separator_arrow, coupling, arrow_factor, arrow_tip, inverse_gram):
    next_cov, next_arrow = passed_along((separator_cov[0], separator_arrow[0]), "tm", -1)
    factor = coupling[0]
    arrow_rows = arrow_factor[0]
    height = factor.shape[0]
    offset = lax.axis_index("panel") * height
    product = matmul(next_cov, lax.all_gather(factor, "panel", axis=0, tiled=True))
    mine_arrow = lax.dynamic_slice_in_dim(next_arrow, offset, height, 1)
    arrow_prod = lax.psum(matmul(mine_arrow, factor), "panel")
    arrow_out = -(arrow_prod + matmul(arrow_tip, arrow_rows))
    own_next_arrow = lax.dynamic_slice_in_dim(next_arrow, offset, height, 1)
    lower = -(product + inner_rows(own_next_arrow, arrow_rows))
    folded = lax.psum_scatter(inner_rows(factor, lower), "panel", scatter_dimension=0, tiled=True)
    own_arrow_rows = lax.dynamic_slice_in_dim(arrow_rows, offset, height, 1)
    diag_out = inverse_gram[0] - folded - inner_rows(own_arrow_rows, arrow_out)
    arrow_share = lax.dynamic_slice_in_dim(arrow_out, offset, height, 1)
    return (diag_out[None], lower[None], arrow_share[None])


def solution(mesh):
    return jax.shard_map(
        per_device,
        mesh=mesh,
        in_specs=(
            P("tm", "panel", None),
            P("tm", None, None),
            P("tm", "panel", None),
            P("tm", None, None),
            P(),
            P("tm", "panel", None),
        ),
        out_specs=(P("tm", "panel", None), P("tm", "panel", None), P("tm", None, "panel")),
        check_vma=False,
    )
```

profile of v0, /device:TPU:0, one launch (start us, length us, event | category | flops | bytes accessed | tf_op | source)
XLA Modules:
  0.0 272.7 jit_solution(7942340729840633537)
XLA Ops:
  7.2 0.0 copy-start
  7.2 0.0 copy-start.1
  7.2 0.0 all-gather.3.cloned.1.call-start
  7.2 0.7 all-gather.3.cloned.1.call-update
  7.9 0.0 reduce-scatter.4.cloned.1.call-start
  8.0 1.3 collective-permute-start
  9.3 0.8 copy.31
  10.1 1.3 collective-permute-start.1
  11.4 13.6 %collective-permute-done.1 = f32[6,2048]{1,0:T(8,128)S(1)} collective-permute-done((f32[6,2048]{1,0:T(8,128)S(1)}, f32[6,2048]{1,0:T(8,128)S(1)}, u32[]{:S(2)}, u32[]{:S(2)}) %collective-permute-start.1) | collective-permute-done | bytes 49184 | tf_op jit(solution)/shard_map/ppermute | solution.py:12
  25.0 1.5 fusion.14
  26.5 0.0 collective-permute-done
  26.5 58.9 %all-gather.3.cloned.1.call-done = f32[1,2048,2048]{2,1,0:T(8,128)} async-done(((f32[1,64,2048]{2,1,0:T(8,128)}), f32[1,2048,2048]{2,1,0:T(8,128)}) %all-gather.3.cloned.1.call-update) | async-done | bytes 16777232 | tf_op jit(solution)/shard_map/all_gather | solution.py:31
  85.5 13.8 %fusion.6 = f32[64,2048]{1,0:T(8,128)S(1)} fusion(f32[64,2048]{1,0:T(8,128)S(1)} %fusion.14, f32[64,2048]{1,0:T(8,128)S(1)} %collective-permute-done, f32[1,2048,2048]{2,1,0:T(8,128)} %all-gather.3.cloned.1.call-done), kind=kOutput, calls=%fused_computation.6 | convolution fusion | flops 3221487616 | bytes 18350080 | tf_op jit(solution)/shard_map/dot_general | solution.py:16
  99.3 0.0 copy-done.1
  99.3 0.0 copy-start.2
  99.3 16.0 %convolution_bitcast_fusion = f32[2048,2048]{0,1:T(8,128)} fusion(f32[64,2048]{1,0:T(8,128)S(1)} %fusion.6, f32[1,64,2048]{2,1,0:T(8,128)S(1)} %copy-done.1), kind=kOutput, calls=%fused_computation.2 | convolution fusion | flops 3221225472 | bytes 17825792 | tf_op jit(solution)/shard_map/dot_general | solution.py:20
  115.3 17.6 %copy.13 = f32[2048,2048]{1,0:T(8,128)} copy(f32[2048,2048]{0,1:T(8,128)} %convolution_bitcast_fusion) | data formatting | bytes 33554432
  132.9 0.0 copy-done.2
  132.9 0.0 copy-start.4
  132.9 0.0 copy-start.3
  132.9 0.0 reduce-scatter.4.cloned.1.call-update
  132.9 0.8 copy-done.4
  133.7 0.1 constant_dynamic-slice_fusion.1
  133.8 0.0 copy-done
  133.8 0.2 fusion.12
  134.0 0.4 fusion.10
  134.4 128.3 %psum.7 = f32[6,2048]{1,0:T(8,128)S(1)} all-reduce(f32[6,2048]{1,0:T(8,128)S(1)} %fusion.10), channel_id=1, replica_groups=mesh['tm'=4,'panel'=32] {'panel'}, use_global_device_ids=true, to_apply=%region_1.0 | all-reduce | flops 12288 | bytes 98304 | tf_op jit(solution)/shard_map/psum | solution.py:33
  262.7 0.1 constant_dynamic-slice_fusion
  262.8 0.6 broadcast_in_dim.11
  263.4 0.0 reduce-scatter.4.cloned.1.call-done
  263.4 0.0 copy-done.3
  263.4 2.5 fusion.2
  (1 shorter events, 0.0 us)
Async XLA Ops:
  7.2 126.6 %copy-start = (f32[6,6]{1,0:T(8,128)S(1)}, f32[6,6]{1,0:T(8,128)}, u32[]{:S(2)}) copy-start(f32[6,6]{1,0:T(8,128)} %param.10) | copy-start | bytes 436
  7.2 92.1 %copy-start.1 = (f32[1,64,2048]{2,1,0:T(8,128)S(1)}, f32[1,64,2048]{2,1,0:T(8,128)}, u32[]{:S(2)}) copy-start(f32[1,64,2048]{2,1,0:T(8,128)} %param.8) | copy-start | bytes 1572868
  7.2 78.3 %all-gather.3.cloned.1.call-start = ((), (), s32[]{:S(2)}) async-start(), calls=%async_computation.1 | async-start | bytes 17301504 | tf_op jit(solution)/shard_map/all_gather | solution.py:31
  7.9 255.4 %reduce-scatter.4.cloned.1.call-start = ((), (), s32[]{:S(2)}) async-start(), calls=%async_computation.2 | async-start | bytes 17301504 | tf_op jit(solution)/shard_map/reduce_scatter | solution.py:37
  8.0 18.6 %collective-permute-start = (f32[64,2048]{1,0:T(8,128)}, f32[64,2048]{1,0:T(8,128)S(1)}, u32[]{:S(2)}, u32[]{:S(2)}) collective-permute-start(f32[64,2048]{1,0:T(8,128)} %bitcast.40), channel_id=1, source_target_pairs={{32,0},{64,32},{96,64},{33,1},{65,33},{97,65},{34,2},{66,34},{98,6... | collective-permute-start | bytes 1572872 | tf_op jit(solution)/shard_map/ppermute | solution.py:12
  10.1 14.9 %collective-permute-start.1 = (f32[6,2048]{1,0:T(8,128)S(1)}, f32[6,2048]{1,0:T(8,128)S(1)}, u32[]{:S(2)}, u32[]{:S(2)}) collective-permute-start(f32[6,2048]{1,0:T(8,128)S(1)} %bitcast.39), channel_id=1, source_target_pairs={{32,0},{64,32},{96,64},{33,1},{65,33},{97,65},{34,2},{66,34},{98,6... | collective-permute-start | bytes 147464 | tf_op jit(solution)/shard_map/ppermute | solution.py:12
  99.3 33.6 %copy-start.2 = (f32[64,2048]{1,0:T(8,128)}, f32[64,2048]{1,0:T(8,128)S(1)}, u32[]{:S(2)}) copy-start(f32[64,2048]{1,0:T(8,128)S(1)} %fusion.6) | copy-start | bytes 1572868
  132.9 0.8 copy-start.4
  132.9 130.5 %copy-start.3 = (f32[1,64,2048]{2,1,0:T(8,128)S(1)}, f32[1,64,2048]{2,1,0:T(8,128)}, u32[]{:S(2)}) copy-start(f32[1,64,2048]{2,1,0:T(8,128)} %param.11) | copy-start | bytes 1572868
Sparse Core Ops, SparseCore 0:
  10.3 75.1 all-gather.2
  133.1 115.5 reduce-scatter.3
where the time goes:
time: 273 us
  blocking collectives  128 us (47%)
  waiting for transfers between devices  73.2 us (27%)
  matrix products  34.4 us (13%)
  local copies, waits for them, and re-layouts  19.9 us (7%)
  between operations  14.1 us (5%)
    psum x1, blocking collectives, per_device(): arrow_prod = lax.psum(matmul(mine_arrow, factor), 'panel')  128 us
    all_gather x1, waiting for transfers between devices, per_device(): lax.all_gather(factor, 'panel', axis=0, tiled=True)  58.9 us
    dot_general x3, matrix products, inner_rows(): lax.dot_general(left, right, (((0,), (0,)), ((), ())), preferred_element_...  20 us
    unnamed x12, local copies, waits for them, and re-layouts  19.2 us
    dot_general x3, matrix products, matmul(): jnp.dot(left, right, preferred_element_type=jnp.float32, precision=hp)  14.4 us
    ppermute x2, waiting for transfers between devices, passed_along(): return lax.ppermute(block, axis, route)  13.6 us
  transfers between devices with their start and end apart: 4, of which 2 were waited for; matrix products, arithmetic and copies ran while one was open for 1% of the time, Pallas kernels for 0%

commit v1 on v0

--- a/solution.py
+++ b/solution.py
@@ -1,9 +1,25 @@
+import functools
 import jax
 import jax.numpy as jnp
 from jax import lax
 from jax.sharding import PartitionSpec as P
 
 hp = lax.Precision.HIGHEST
+
+
+def area_switch(v0, axis_name):
+    return jnp.concatenate(
+        lax.all_to_all(
+            jnp.stack([v0 for _ in range(lax.axis_size(axis_name))]),
+            axis_name,
+            concat_axis=0,
+            split_axis=0,
+        ),
+        axis=0,
+    )
+
+
+group_copies = functools.partial(area_switch, axis_name="panel")
 
 
 def passed_along(block, axis, distance):
@@ -28,7 +44,7 @@
     arrow_rows = arrow_factor[0]
     height = factor.shape[0]
     offset = lax.axis_index("panel") * height
-    product = matmul(next_cov, lax.all_gather(factor, "panel", axis=0, tiled=True))
+    product = matmul(next_cov, group_copies(factor))
     mine_arrow = lax.dynamic_slice_in_dim(next_arrow, offset, height, 1)
     arrow_prod = lax.psum(matmul(mine_arrow, factor), "panel")
     arrow_out = -(arrow_prod + matmul(arrow_tip, arrow_rows))

time: 273 us -> 473 us (1.73)
  waiting for transfers between devices: 73.2 us -> 237 us
  blocking collectives: 128 us -> 149 us
  starting transfers between devices: 2.66 us -> 11.5 us
  local copies, waits for them, and re-layouts: 19.9 us -> 27.4 us
    all_to_all x0 -> x1, waiting for transfers between devices: none -> 222 us  [area_switch(): lax.all_to_all(jnp.stack([v0 for _ in range(lax.axis_size(axis_name))]),...]
    all_gather x1 -> x0, waiting for transfers between devices: 58.9 us -> none  [per_device(): lax.all_gather(factor, 'panel', axis=0, tiled=True)]
    psum x1, blocking collectives: 128 us -> 149 us  [per_device(): arrow_prod = lax.psum(matmul(mine_arrow, factor), 'panel')]
    another operation x0 -> x1, local copies, waits for them, and re-layouts: none -> 8.93 us  [area_switch(): jnp.stack([v0 for _ in range(lax.axis_size(axis_name))])]
    all_to_all x0 -> x1, starting transfers between devices: none -> 8.71 us  [area_switch(): lax.all_to_all(jnp.stack([v0 for _ in range(lax.axis_size(axis_name))]),...]
    unnamed x12 -> x16, local copies, waits for them, and re-layouts: 19.2 us -> 17.7 us
  transfers between devices with their start and end apart: 4 -> 4, of which waited for: 2 -> 2; matrix products, arithmetic and copies ran while one was open for 1% -> 0% of each run, Pallas kernels for 0% -> 0%
where the time goes in v1:
time: 473 us
  waiting for transfers between devices  237 us (50%)
  blocking collectives  149 us (32%)
  matrix products  33.7 us (7%)
  local copies, waits for them, and re-layouts  27.4 us (6%)
  between operations  14.2 us (3%)
  starting transfers between devices  11.5 us (2%)
    all_to_all x1, waiting for transfers between devices, area_switch(): lax.all_to_all(jnp.stack([v0 for _ in range(lax.axis_size(axis_name))]),...  222 us
    psum x1, blocking collectives, per_device(): arrow_prod = lax.psum(matmul(mine_arrow, factor), 'panel')  149 us
    dot_general x3, matrix products, inner_rows(): lax.dot_general(left, right, (((0,), (0,)), ((), ())), preferred_element_...  19.3 us
    unnamed x16, local copies, waits for them, and re-layouts  17.7 us
    ppermute x2, waiting for transfers between devices, passed_along(): return lax.ppermute(block, axis, route)  14.7 us
    dot_general x3, matrix products, matmul(): jnp.dot(left, right, preferred_element_type=jnp.float32, precision=hp)  14.4 us
  transfers between devices with their start and end apart: 4, of which 2 were waited for; matrix products, arithmetic and copies ran while one was open for 0% of the time, Pallas kernels for 0%

profile of v1, /device:TPU:0, one launch (start us, length us, event | category | flops | bytes accessed | tf_op | source)
XLA Modules:
  0.0 472.8 jit_solution(8523424194310628522)
XLA Ops:
  7.2 0.0 copy-start
  7.2 8.9 %stack.3 = f32[32,64,2048]{2,1,0:T(8,128)} broadcast(f32[64,2048]{1,0:T(8,128)} %bitcast.33), dimensions={1,2} | broadcast | bytes 17301504 | tf_op jit(solution)/shard_map/stack | solution.py:13
  16.1 0.0 copy-start.6
  16.1 0.0 copy-start.5
  16.1 0.0 copy-start.4
  16.1 8.7 %all-to-all-start = ((f32[32,64,2048]{2,1,0:T(8,128)}), f32[32,64,2048]{2,1,0:T(8,128)}, u32[]{:S(2)}, u32[]{:S(2)}) async-start(f32[32,64,2048]{2,1,0:T(8,128)} %stack.3), calls=%async_computation | async-start | bytes 33554432 | tf_op jit(solution)/shard_map/all_to_all | solution.py:12
  24.8 0.0 copy-start.1
  24.8 0.0 reduce-scatter.4.cloned.1.call-start
  24.9 0.0 copy-done.6
  24.9 1.4 collective-permute-start
  26.3 0.0 copy-done.5
  26.4 1.3 collective-permute-start.1
  27.7 14.7 %collective-permute-done.1 = f32[6,2048]{1,0:T(8,128)S(1)} collective-permute-done((f32[6,2048]{1,0:T(8,128)S(1)}, f32[6,2048]{1,0:T(8,128)S(1)}, u32[]{:S(2)}, u32[]{:S(2)}) %collective-permute-start.1) | collective-permute-done | bytes 49184 | tf_op jit(solution)/shard_map/ppermute | solution.py:28
  42.4 0.0 copy-done.4
  42.4 0.7 fusion.4
  43.1 0.0 collective-permute-done
  43.1 221.9 %all-to-all-done = f32[32,64,2048]{2,1,0:T(8,128)} async-done(((f32[32,64,2048]{2,1,0:T(8,128)}), f32[32,64,2048]{2,1,0:T(8,128)}, u32[]{:S(2)}, u32[]{:S(2)}) %all-to-all-start) | async-done | bytes 16777248 | tf_op jit(solution)/shard_map/all_to_all | solution.py:12
  265.0 13.8 %fusion.1 = f32[64,2048]{1,0:T(8,128)S(1)} fusion(f32[64,2048]{1,0:T(8,128)S(1)} %fusion.4, f32[64,2048]{1,0:T(8,128)S(1)} %collective-permute-done, f32[2048,2048]{1,0:T(8,128)} %bitcast.3), kind=kOutput, calls=%fused_computation.4 | convolution fusion | flops 3221487616 | bytes 18350080 | tf_op jit(solution)/shard_map/dot_general | solution.py:32
  278.9 0.0 copy-done.1
  278.9 0.0 copy-start.2
  278.9 16.1 %convolution_bitcast_fusion = f32[2048,2048]{0,1:T(8,128)} fusion(f32[64,2048]{1,0:T(8,128)S(1)} %fusion.1, f32[1,64,2048]{2,1,0:T(8,128)S(1)} %copy-done.1), kind=kOutput, calls=%fused_computation | convolution fusion | flops 3221225472 | bytes 17825792 | tf_op jit(solution)/shard_map/dot_general | solution.py:36
  295.0 17.6 %copy.13 = f32[2048,2048]{1,0:T(8,128)} copy(f32[2048,2048]{0,1:T(8,128)} %convolution_bitcast_fusion) | data formatting | bytes 33554432
  312.6 0.0 copy-done.2
  312.6 0.0 copy-start.3
  312.6 0.0 reduce-scatter.4.cloned.1.call-update
  312.7 0.1 constant_dynamic-slice_fusion.1
  312.7 0.0 copy-done
  312.7 0.2 fusion.2
  312.9 0.4 fusion.10
  313.3 149.5 %psum.7 = f32[6,2048]{1,0:T(8,128)S(1)} all-reduce(f32[6,2048]{1,0:T(8,128)S(1)} %fusion.10), channel_id=1, replica_groups=mesh['tm'=4,'panel'=32] {'panel'}, use_global_device_ids=true, to_apply=%region_1.0 | all-reduce | flops 12288 | bytes 98304 | tf_op jit(solution)/shard_map/psum | solution.py:49
  462.8 0.1 constant_dynamic-slice_fusion
  462.9 0.6 broadcast_in_dim.11
  463.4 0.0 reduce-scatter.4.cloned.1.call-done
  463.4 0.0 copy-done.3
  463.4 2.5 fusion
  (2 shorter events, 0.0 us)
Async XLA Ops:
  7.2 305.6 %copy-start = (f32[6,6]{1,0:T(8,128)S(1)}, f32[6,6]{1,0:T(8,128)}, u32[]{:S(2)}) copy-start(f32[6,6]{1,0:T(8,128)} %param.10) | copy-start | bytes 436
  16.1 8.8 %copy-start.6 = (f32[1,64,2048]{2,1,0:T(8,128)S(1)}, f32[1,64,2048]{2,1,0:T(8,128)}, u32[]{:S(2)}) copy-start(f32[1,64,2048]{2,1,0:T(8,128)} %param.6) | copy-start | bytes 1572868
  16.1 10.2 %copy-start.5 = (f32[1,6,2048]{2,0,1:T(1,128)S(1)}, f32[1,6,2048]{2,0,1:T(1,128)}, u32[]{:S(2)}) copy-start(f32[1,6,2048]{2,0,1:T(1,128)} %param.7) | copy-start | bytes 147460
  16.1 26.2 %copy-start.4 = (f32[1,6,2048]{2,0,1:T(1,128)S(1)}, f32[1,6,2048]{2,0,1:T(1,128)}, u32[]{:S(2)}) copy-start(f32[1,6,2048]{2,0,1:T(1,128)} %param.9) | copy-start | bytes 147460
  16.1 248.9 %all-to-all-start = ((f32[32,64,2048]{2,1,0:T(8,128)}), f32[32,64,2048]{2,1,0:T(8,128)}, u32[]{:S(2)}, u32[]{:S(2)}) async-start(f32[32,64,2048]{2,1,0:T(8,128)} %stack.3), calls=%async_computation | async-start | bytes 33554432 | tf_op jit(solution)/shard_map/all_to_all | solution.py:12
  24.8 254.1 %copy-start.1 = (f32[1,64,2048]{2,1,0:T(8,128)S(1)}, f32[1,64,2048]{2,1,0:T(8,128)}, u32[]{:S(2)}) copy-start(f32[1,64,2048]{2,1,0:T(8,128)} %param.8) | copy-start | bytes 1572868
  24.8 438.6 %reduce-scatter.4.cloned.1.call-start = ((), (), s32[]{:S(2)}) async-start(), calls=%async_computation.2 | async-start | bytes 17301504 | tf_op jit(solution)/shard_map/reduce_scatter | solution.py:53
  24.9 18.2 %collective-permute-start = (f32[64,2048]{1,0:T(8,128)S(1)}, f32[64,2048]{1,0:T(8,128)S(1)}, u32[]{:S(2)}, u32[]{:S(2)}) collective-permute-start(f32[64,2048]{1,0:T(8,128)S(1)} %bitcast.36), channel_id=1, source_target_pairs={{32,0},{64,32},{96,64},{33,1},{65,33},{97,65},{34,2},{66,34},{98,6... | collective-permute-start | bytes 1572872 | tf_op jit(solution)/shard_map/ppermute | solution.py:28
  26.4 16.0 %collective-permute-start.1 = (f32[6,2048]{1,0:T(8,128)S(1)}, f32[6,2048]{1,0:T(8,128)S(1)}, u32[]{:S(2)}, u32[]{:S(2)}) collective-permute-start(f32[6,2048]{1,0:T(8,128)S(1)} %bitcast.35), channel_id=1, source_target_pairs={{32,0},{64,32},{96,64},{33,1},{65,33},{97,65},{34,2},{66,34},{98,6... | collective-permute-start | bytes 147464 | tf_op jit(solution)/shard_map/ppermute | solution.py:28
  278.9 33.7 %copy-start.2 = (f32[64,2048]{1,0:T(8,128)}, f32[64,2048]{1,0:T(8,128)S(1)}, u32[]{:S(2)}) copy-start(f32[64,2048]{1,0:T(8,128)S(1)} %fusion.1) | copy-start | bytes 1572868
  312.6 150.8 %copy-start.3 = (f32[1,64,2048]{2,1,0:T(8,128)S(1)}, f32[1,64,2048]{2,1,0:T(8,128)}, u32[]{:S(2)}) copy-start(f32[1,64,2048]{2,1,0:T(8,128)} %param.11) | copy-start | bytes 1572868
Sparse Core Ops, SparseCore 0:
  312.8 144.7 reduce-scatter.3
